TPU v7x, 32 devices: a whole 2x2x4 slice. The times are simulated.
32 devices in a mesh: dp: 4 (over x, core), seq: 8 (over z, y).
Axes of the slice: x: 2, y: 2, z: 4, core: 2. Of those that a mesh axis runs over, the one named last changes fastest.
Arguments:
- queries: bfloat16 [8192, 16, 128], P(('dp', 'seq')), parts along dimension 0, may hold values from -6 to 6
- keys: bfloat16 [8192, 16, 128], P(('dp', 'seq')), parts along dimension 0, may hold values from -6 to 6
- values: bfloat16 [8192, 16, 128], P(('dp', 'seq')), parts along dimension 0, may hold values from -6 to 6
- cotangent: bfloat16 [8192, 16, 128], P(('dp', 'seq')), parts along dimension 0, may hold values from -6 to 6
- doc_lengths: int32 [96], P('dp'), parts along dimension 0, may hold values from 1 to 512, 2048 in all
Outputs:
- attended: bfloat16 [8192, 16, 128], P(('dp', 'seq')), parts along dimension 0
- grad_queries: bfloat16 [8192, 16, 128], P(('dp', 'seq')), parts along dimension 0
- grad_keys: bfloat16 [8192, 16, 128], P(('dp', 'seq')), parts along dimension 0
- grad_values: bfloat16 [8192, 16, 128], P(('dp', 'seq')), parts along dimension 0
There are 4 independent parts, one for each index of `dp`. A program takes and returns all parts, laid end to end along the dimension named above; each array names one. Nothing has to cross between parts.
Inputs may be any that keep to these rules, and one draw needn't show every extreme that they name: `doc_lengths`: the lengths sum to 2048, and the longest document has exactly 512 positions.
All inputs are finite; a program needn't handle non-finite values.
Results may differ from a plain program's by a relative error of at most 0.005.
Values sent between devices are 32-bit elements; how exact they have to be, the bound alone decides.
A program may use at most 64 MiB of HBM per device.

v0:
```python
import functools

import jax
import jax.numpy as jnp
from jax import lax
from jax.experimental import pallas as pl
from jax.experimental.pallas import tpu as pltpu
from jax.sharding import PartitionSpec as P

BLOCK = 256
LONGEST_PART = 4
MESH = pl.DeviceIdType.MESH


def dot(a, b, ca, cb):
    return lax.dot_general(
        a, b, (((ca,), (cb,)), ((), ())), preferred_element_type=jnp.float32
    )


def kernel(
    seq, hops,
    lengths, q_hbm, k_hbm, v_hbm, c_hbm,
    att_out, gq_out, gk_out, gv_out,
    q_in, k_in, v_in, c_in, qf, kf, vf, cf, qh, kh, vh, ch,
    mask, state, ret, state_in, ret_in, relay_in,
    load_sem, relay_send, relay_recv, state_send, state_recv, ret_send, ret_recv,
):
    rows, heads, width = q_in.shape
    loads = [
        pltpu.make_async_copy(src, dst, load_sem.at[i])
        for i, (src, dst) in enumerate(
            ((k_hbm, k_in), (v_hbm, v_in), (q_hbm, q_in), (c_hbm, c_in))
        )
    ]
    for load in loads:
        load.start()
    factor = (width * BLOCK) ** (-0.5)
    dp, me = lax.axis_index("dp"), lax.axis_index("seq")
    first = me * rows
    last = first + rows - 1

    barrier = pltpu.get_barrier_semaphore()
    for d in range(1, hops + 1):
        for ok, peer in ((me + d < seq, me + d), (me - d >= 0, me - d)):
            @pl.when(ok)
            def _(peer=peer):
                pl.semaphore_signal(barrier, inc=1, device_id=(dp, peer), device_id_type=MESH)

    for d in range(hops):
        @pl.when(me - d - 1 < 0)
        def _(d=d):
            state_in[d] = jnp.zeros(state_in.shape[1:], state_in.dtype)

        @pl.when(me + d + 1 >= seq)
        def _(d=d):
            ret_in[d] = jnp.zeros(ret_in.shape[1:], ret_in.dtype)

    big = jnp.int32(2**30)
    zero = jnp.int32(0)
    ends = []
    total = zero
    for j in range(lengths.shape[0]):
        total = total + lengths[j]
        ends.append(total)

    def start_of(p):
        out = zero
        for e in ends:
            out = jnp.maximum(out, jnp.where(e <= p, e, zero))
        return out

    def end_of(p):
        out = big
        for e in ends:
            out = jnp.minimum(out, jnp.where(e > p, e, big))
        return out

    tail_start = start_of(last + 1)
    head_end_prev = end_of(first - 1)
    head_start, head_end = start_of(first), end_of(first)
    last_start, last_end = start_of(last), end_of(last)

    step = 16

    def widen(*pairs):
        def part(i, _):
            at = pl.multiple_of(i * step, step)
            for src, dst in pairs:
                block = src[pl.ds(at, step)].astype(jnp.float32)
                dst[pl.ds(at * heads, step * heads), :] = block.reshape(step * heads, width)
            return 0

        lax.fori_loop(0, rows // step, part, 0)

    pl.semaphore_wait(barrier, jnp.minimum(me, hops) + jnp.minimum(seq - 1 - me, hops))

    pos = first + lax.broadcasted_iota(jnp.int32, (rows, width), 0)
    in_tail = pos >= tail_start
    in_head = pos < head_end_prev

    def forward(d, h):
        return pltpu.make_async_remote_copy(
            src_ref=state.at[h], dst_ref=state_in.at[d, h],
            send_sem=state_send.at[d, h], recv_sem=state_recv.at[d, h],
            device_id=(dp, me + d + 1), device_id_type=MESH,
        )

    def backward(d, h):
        return pltpu.make_async_remote_copy(
            src_ref=ret.at[h], dst_ref=ret_in.at[d, h],
            send_sem=ret_send.at[d, h], recv_sem=ret_recv.at[d, h],
            device_id=(dp, me - d - 1), device_id_type=MESH,
        )

    levels = max(seq // 2, 1)
    odd = lax.rem(me, 2) == 1
    even = lax.rem(me, 2) == 0
    level = me // 2
    up, down = me + 1 < seq, me >= 1

    def state_turn(h):
        return lax.rem(h, levels) < levels - 1 - level

    def ret_turn(h):
        return lax.rem(h, levels) < level

    def state_via(h):
        return odd & up & state_turn(h)

    def state_relays(h):
        return even & (me + 2 < seq) & state_turn(h)

    def ret_via(h):
        return even & (me >= 2) & up & ret_turn(h)

    def ret_relays(h):
        return odd & (me >= 2) & ret_turn(h)

    def via_state(h):
        return pltpu.make_async_remote_copy(
            src_ref=state.at[h], dst_ref=relay_in.at[0, h],
            send_sem=state_send.at[0, h], recv_sem=relay_recv.at[0, h],
            device_id=(dp, me - 1), device_id_type=MESH,
        )

    def via_ret(h):
        return pltpu.make_async_remote_copy(
            src_ref=ret.at[h], dst_ref=relay_in.at[1, h],
            send_sem=ret_send.at[0, h], recv_sem=relay_recv.at[1, h],
            device_id=(dp, me + 1), device_id_type=MESH,
        )

    def relay_state(h):
        return pltpu.make_async_remote_copy(
            src_ref=relay_in.at[0, h], dst_ref=state_in.at[0, h],
            send_sem=relay_send.at[0, h], recv_sem=state_recv.at[0, h],
            device_id=(dp, me + 2), device_id_type=MESH,
        )

    def relay_ret(h):
        return pltpu.make_async_remote_copy(
            src_ref=relay_in.at[1, h], dst_ref=ret_in.at[0, h],
            send_sem=relay_send.at[1, h], recv_sem=ret_recv.at[0, h],
            device_id=(dp, me - 2), device_id_type=MESH,
        )

    def sends_state(d, h):
        if d == 0 and hops > 1:
            return up & jnp.logical_not(state_via(h))
        return me + d + 1 < seq

    def sends_ret(d, h):
        if d == 0 and hops > 1:
            return down & jnp.logical_not(ret_via(h))
        return me - d - 1 >= 0

    def arrived_state(h):
        return pltpu.make_async_remote_copy(
            src_ref=state.at[h], dst_ref=relay_in.at[0, h],
            send_sem=state_send.at[0, h], recv_sem=relay_recv.at[0, h],
            device_id=(dp, me + 1), device_id_type=MESH,
        )

    def arrived_ret(h):
        return pltpu.make_async_remote_copy(
            src_ref=ret.at[h], dst_ref=relay_in.at[1, h],
            send_sem=ret_send.at[0, h], recv_sem=relay_recv.at[1, h],
            device_id=(dp, me - 1), device_id_type=MESH,
        )

    def relay(h):
        if hops > 1:
            @pl.when(state_relays(h))
            def _():
                arrived_state(h).wait_recv()
                relay_state(h).start()

            @pl.when(ret_relays(h))
            def _():
                arrived_ret(h).wait_recv()
                relay_ret(h).start()

    def state_sum(h):
        k32 = kf[pl.ds(h, rows, stride=heads), :]
        v16 = vf[pl.ds(h, rows, stride=heads), :].astype(jnp.bfloat16)
        kh[h] = k32.astype(jnp.bfloat16)
        vh[h] = v16
        state[h] = dot(jnp.where(in_tail, k32, 0.0).astype(jnp.bfloat16), v16, 0, 0)
        if hops > 1:
            @pl.when(state_via(h))
            def _():
                via_state(h).start()

        for d in range(hops):
            @pl.when(sends_state(d, h))
            def _(d=d):
                forward(d, h).start()

    def ret_sum(h):
        q32 = qf[pl.ds(h, rows, stride=heads), :]
        c16 = cf[pl.ds(h, rows, stride=heads), :].astype(jnp.bfloat16)
        qh[h] = q32.astype(jnp.bfloat16)
        ch[h] = c16
        ret[h] = dot(jnp.where(in_head, q32, 0.0).astype(jnp.bfloat16), c16, 0, 0)
        if hops > 1:
            @pl.when(ret_via(h))
            def _():
                via_ret(h).start()

        for d in range(hops):
            @pl.when(sends_ret(d, h))
            def _(d=d):
                backward(d, h).start()

    def each(fn):
        def body(h, _):
            fn(h)
            return 0

        return body

    ahead = min(4, heads)
    loads[0].wait()
    loads[1].wait()
    widen((k_in, kf), (v_in, vf))
    lax.fori_loop(0, ahead, each(state_sum), 0)
    loads[2].wait()
    loads[3].wait()
    widen((q_in, qf), (c_in, cf))

    def both(h):
        ret_sum(h)
        state_sum(h + ahead)

    lax.fori_loop(0, heads - ahead, each(both), 0)
    lax.fori_loop(heads - ahead, heads, each(ret_sum), 0)

    t_pos = first + lax.broadcasted_iota(jnp.int32, (rows, rows), 0)
    s_pos = first + lax.broadcasted_iota(jnp.int32, (rows, rows), 1)
    col = first + lax.broadcasted_iota(jnp.int32, (rows, 1), 0)
    begin = jnp.zeros((rows, 1), jnp.int32)
    for e in ends:
        begin = jnp.maximum(begin, jnp.where(col >= e, e, 0))
    visible = (s_pos <= t_pos) & (s_pos >= begin)
    mask[...] = jnp.where(visible, factor, 0.0).astype(jnp.float32)

    lead = heads // 8

    def inside(h, _):
        @pl.when(h >= heads // 2 - lead)
        def _():
            relay(h - (heads // 2 - lead))

        q, k, v, c = qh[h], kh[h], vh[h], ch[h]
        m = mask[...]
        weights = (m * dot(q, k, 1, 1)).astype(jnp.bfloat16)
        grad_weights = (m * dot(c, v, 1, 1)).astype(jnp.bfloat16)
        spot = pl.ds(h, rows, stride=heads)
        qf[spot, :] = dot(weights, v, 1, 0)
        kf[spot, :] = dot(grad_weights, k, 1, 0)
        vf[spot, :] = dot(grad_weights, q, 0, 0)
        cf[spot, :] = dot(weights, c, 0, 0)
        return 0

    lax.fori_loop(0, heads, inside, 0)

    head_factor = jnp.where(pos < head_end, factor, 0.0).astype(jnp.float32)
    tail_factor = jnp.where(pos >= last_start, factor, 0.0).astype(jnp.float32)

    def outside(h, _):
        carried = jnp.zeros((width, width), jnp.float32)
        returned = jnp.zeros((width, width), jnp.float32)
        @pl.when((h >= heads - heads // 2) & (h + lead < heads))
        def _():
            relay(h + lead)

        for d in range(hops):
            @pl.when(me - d - 1 >= 0)
            def _(d=d):
                forward(d, h).wait_recv()

            @pl.when(me + d + 1 < seq)
            def _(d=d):
                backward(d, h).wait_recv()

            here = head_start <= first - d * rows
            carried = carried + jnp.where(here, state_in[d, h], 0.0)
            there = last_end >= last + d * rows + 1
            returned = returned + jnp.where(there, ret_in[d, h], 0.0)
        carried = carried.astype(jnp.bfloat16)
        returned = returned.astype(jnp.bfloat16)
        q, k, v, c = qh[h], kh[h], vh[h], ch[h]
        spot = pl.ds(h, rows, stride=heads)
        qf[spot, :] = qf[spot, :] + head_factor * dot(q, carried, 1, 0)
        kf[spot, :] = kf[spot, :] + head_factor * dot(c, carried, 1, 1)
        vf[spot, :] = vf[spot, :] + tail_factor * dot(v, returned, 1, 1)
        cf[spot, :] = cf[spot, :] + tail_factor * dot(k, returned, 1, 0)
        return 0

    lax.fori_loop(0, heads, outside, 0)

    def narrow(i, _):
        at = pl.multiple_of(i * step, step)
        for src, dst in ((qf, att_out), (kf, gq_out), (vf, gk_out), (cf, gv_out)):
            block = src[pl.ds(at * heads, step * heads), :].reshape(step, heads, width)
            dst[pl.ds(at, step)] = block.astype(jnp.bfloat16)
        return 0

    lax.fori_loop(0, rows // step, narrow, 0)

    def drain(h):
        for d in range(hops):
            @pl.when(sends_state(d, h))
            def _(d=d):
                forward(d, h).wait_send()

            @pl.when(sends_ret(d, h))
            def _(d=d):
                backward(d, h).wait_send()

        if hops > 1:
            @pl.when(state_via(h))
            def _():
                via_state(h).wait_send()

            @pl.when(ret_via(h))
            def _():
                via_ret(h).wait_send()

            @pl.when(state_relays(h))
            def _():
                relay_state(h).wait_send()

            @pl.when(ret_relays(h))
            def _():
                relay_ret(h).wait_send()

    lax.fori_loop(0, heads, each(drain), 0)


def local(seq, queries, keys, values, cotangent, doc_lengths):
    rows, heads, width = queries.shape
    longest = seq * rows // LONGEST_PART
    hops = min(seq - 1, (longest - 1 + rows - 1) // rows)
    vmem = pl.BlockSpec(memory_space=pltpu.VMEM)
    flat = pltpu.VMEM((rows * heads, width), jnp.float32)
    by_head = pltpu.VMEM((heads, rows, width), jnp.bfloat16)
    whole = pltpu.VMEM((rows, heads, width), jnp.bfloat16)
    square = pltpu.VMEM((heads, width, width), jnp.float32)
    squares = pltpu.VMEM((hops, heads, width, width), jnp.float32)
    return pl.pallas_call(
        functools.partial(kernel, seq, hops),
        out_shape=[jax.ShapeDtypeStruct(queries.shape, jnp.bfloat16)] * 4,
        in_specs=[pl.BlockSpec(memory_space=pltpu.SMEM)]
        + [pl.BlockSpec(memory_space=pltpu.HBM)] * 4,
        out_specs=[vmem] * 4,
        scratch_shapes=[whole] * 4
        + [flat] * 4
        + [by_head] * 4
        + [pltpu.VMEM((rows, rows), jnp.float32), square, square, squares, squares,
           pltpu.VMEM((2, heads, width, width), jnp.float32)]
        + [pltpu.SemaphoreType.DMA((4,)), pltpu.SemaphoreType.DMA((2, heads)), pltpu.SemaphoreType.DMA((2, heads))]
        + [pltpu.SemaphoreType.DMA((hops, heads))] * 4,
        compiler_params=pltpu.CompilerParams(
            collective_id=0, has_side_effects=True, vmem_limit_bytes=49 * 2**20
        ),
    )(doc_lengths, queries, keys, values, cotangent)


def solution(mesh):
    spec = P(("dp", "seq"), None, None)
    return jax.shard_map(
        functools.partial(local, mesh.shape["seq"]),
        mesh=mesh,
        in_specs=(spec, spec, spec, spec, P("dp")),
        out_specs=(spec, spec, spec, spec),
        check_vma=False,
    )
```

profile of v0, /device:TPU:12, one launch (start us, length us, event | category | flops | bytes accessed | tf_op | source)
XLA Modules:
  0.0 57.3 jit_solution(6100616088235777390)
XLA Ops:
  0.6 0.0 copy-start
  0.6 0.6 %copy-done = s32[24]{0:T(128)S(1)} copy-done((s32[24]{0:T(128)S(1)}, s32[24]{0:T(128)}, u32[]{:S(2)}) %copy-start) | copy-done | bytes 120
  1.3 52.1 %shard_map.84 = (bf16[256,16,128]{2,1,0:T(8,128)(2,1)S(1)}, bf16[256,16,128]{2,1,0:T(8,128)(2,1)S(1)}, bf16[256,16,128]{2,1,0:T(8,128)(2,1)S(1)}, bf16[256,16,128]{2,1,0:T(8,128)(2,1)S(1)}) custom-call(s32[24]{0:T(128)S(1)} %copy-done, bf16[256,16,128]{2,1,0:T(8,128)(2,1)} %q_hbm.1, bf16[256,16,128]{2,1,0:T(8,128)(2,1)} %k_hbm.1, ...), custom_call_target="tpu_custom_call" | custom-call | tf_op jit(solution)/shard_map/pallas_call | solution.py:372
  53.4 1.0 %copy.13 = bf16[256,16,128]{2,1,0:T(8,128)(2,1)} copy(bf16[256,16,128]{2,1,0:T(8,128)(2,1)S(1)} %get-tuple-element.8) | data formatting | bytes 2097152
  54.4 1.0 %copy.14 = bf16[256,16,128]{2,1,0:T(8,128)(2,1)} copy(bf16[256,16,128]{2,1,0:T(8,128)(2,1)S(1)} %get-tuple-element.9) | data formatting | bytes 2097152
  55.4 1.0 %copy.15 = bf16[256,16,128]{2,1,0:T(8,128)(2,1)} copy(bf16[256,16,128]{2,1,0:T(8,128)(2,1)S(1)} %get-tuple-element.10) | data formatting | bytes 2097152
  56.3 1.0 %copy.16 = bf16[256,16,128]{2,1,0:T(8,128)(2,1)} copy(bf16[256,16,128]{2,1,0:T(8,128)(2,1)S(1)} %get-tuple-element.11) | data formatting | bytes 2097152
Async XLA Ops:
  0.6 0.7 %copy-start = (s32[24]{0:T(128)S(1)}, s32[24]{0:T(128)}, u32[]{:S(2)}) copy-start(s32[24]{0:T(128)} %lengths.1) | copy-start | bytes 292
where the time goes:
time: 57.5 us; the launch traced here: 57.3 us
  Pallas kernels  52.1 us (91%)
  local copies, waits for them, and re-layouts  4.53 us (8%)
  between operations  0.65 us (1%)
    pallas_call x1, Pallas kernels, local(): pl.pallas_call(functools.partial(kernel, seq, hops), out_shape=[jax.Shape...  52.1 us
    unnamed x6, local copies, waits for them, and re-layouts  4.53 us

commit v1 on v0

--- a/solution.py
+++ b/solution.py
@@ -10,6 +10,8 @@
 BLOCK = 256
 LONGEST_PART = 4
 MESH = pl.DeviceIdType.MESH
+INNER_LAG, OUTER_LAG = 3, 5
+LOAD_PARTS, STORE_PARTS = 4, 4
 
 
 def dot(a, b, ca, cb):
@@ -359,10 +361,369 @@
     lax.fori_loop(0, heads, each(drain), 0)
 
 
+def paired(
+    seq,
+    lens_hbm, q_hbm, k_hbm, v_hbm, c_hbm,
+    o1, o2, o3, o4,
+    lengths, xa_in, xb_in, pa_in, pb_in, xa_h, xb_h, pa_h, pb_h,
+    mask, x_rows, p_rows, x_scale, p_scale,
+    x_out, p_raw, p_sum, near_in, far_in, pair_in, relay_in,
+    len_sem, load_sem, near_send, near_recv, far_send, far_recv,
+    pair_send, pair_recv, relay_send, relay_recv,
+):
+    rows, heads, width = xa_in.shape
+    factor = (width * BLOCK) ** (-0.5)
+    dp, me = lax.axis_index("dp"), lax.axis_index("seq")
+    odd = lax.rem(me, 2) == 1
+    even = jnp.logical_not(odd)
+    toward = jnp.where(odd, 1, -1)
+    first = me * rows
+    last = first + rows - 1
+    parts = load_sem.shape[1]
+    span = rows // parts
+
+    len_load = pltpu.make_async_copy(lens_hbm, lengths, len_sem)
+    len_load.start()
+
+    def load(i, part, src, dst):
+        cut = pl.ds(part * span, span)
+        return pltpu.make_async_copy(src.at[cut], dst.at[cut], load_sem.at[i, part])
+
+    landing = (xa_in, xb_in, pa_in, pb_in)
+
+    @pl.when(even)
+    def _():
+        for pair in (0, 2):
+            for part in range(parts):
+                for i in (pair, pair + 1):
+                    load(i, part, (q_hbm, c_hbm, k_hbm, v_hbm)[i], landing[i]).start()
+
+    @pl.when(odd)
+    def _():
+        for pair in (0, 2):
+            for part in range(parts):
+                for i in (pair, pair + 1):
+                    load(i, part, (k_hbm, v_hbm, q_hbm, c_hbm)[i], landing[i]).start()
+
+    near, pair = me + toward, me - toward
+    far_to, far_from = me - 2 * toward, me + 2 * toward
+    near_ok = (near >= 0) & (near < seq)
+    far_to_ok = (far_to >= 0) & (far_to < seq)
+    far_from_ok = (far_from >= 0) & (far_from < seq)
+
+    barrier = pltpu.get_barrier_semaphore()
+    for ok, peer in ((near_ok, near), (pair >= 0, pair), (far_to_ok, far_to), (far_from_ok, far_from)):
+        @pl.when(ok)
+        def _(peer=peer):
+            pl.semaphore_signal(barrier, inc=1, device_id=(dp, peer), device_id_type=MESH)
+
+    @pl.when(jnp.logical_not(near_ok))
+    def _():
+        near_in[...] = jnp.zeros(near_in.shape, near_in.dtype)
+
+    @pl.when(jnp.logical_not(far_from_ok))
+    def _():
+        far_in[...] = jnp.zeros(far_in.shape, far_in.dtype)
+
+    len_load.wait()
+    big = jnp.int32(2**30)
+    zero = jnp.int32(0)
+    ends = []
+    total = zero
+    for j in range(lengths.shape[0]):
+        total = total + lengths[j]
+        ends.append(total)
+
+    def start_of(p):
+        out = zero
+        for e in ends:
+            out = jnp.maximum(out, jnp.where(e <= p, e, zero))
+        return out
+
+    def end_of(p):
+        out = big
+        for e in ends:
+            out = jnp.minimum(out, jnp.where(e > p, e, big))
+        return out
+
+    tail_start = start_of(last + 1)
+    head_end_prev = end_of(first - 1)
+    head_start, head_end = start_of(first), end_of(first)
+    last_start, last_end = start_of(last), end_of(last)
+    x_keep = jnp.where(odd, last_end >= last + rows + 1, head_start <= first - rows)
+    p_keep = jnp.where(odd, head_end_prev >= last + 1, tail_start <= first)
+
+    pos = first + lax.broadcasted_iota(jnp.int32, (rows, width), 0)
+    x_low, x_high = jnp.where(odd, tail_start, zero), jnp.where(odd, big, head_end_prev)
+    p_low, p_high = jnp.where(odd, zero, tail_start), jnp.where(odd, head_end_prev, big)
+    x_rows[...] = jnp.where((pos >= x_low) & (pos < x_high), 1.0, 0.0).astype(jnp.bfloat16)
+
+    step = 16
+
+    def widen(part, *pairs):
+        def some(i, _):
+            at = pl.multiple_of(part * span + i * step, step)
+            for src, dst in pairs:
+                block = src[pl.ds(at, step)].astype(jnp.float32)
+                dst[pl.ds(at * heads, step * heads), :] = block.reshape(step * heads, width)
+            return 0
+
+        lax.fori_loop(0, span // step, some, 0)
+
+    levels = seq // 2
+    level = me // 2
+    mine = jnp.where(odd, levels - 1 - level, level)
+    theirs = levels - 1 - mine
+
+    def my_turn(h):
+        return lax.rem(h, levels) < mine
+
+    def their_turn(h):
+        return lax.rem(h, levels) < theirs
+
+    def remote(src, dst, send, recv, peer):
+        return pltpu.make_async_remote_copy(
+            src_ref=src, dst_ref=dst, send_sem=send, recv_sem=recv,
+            device_id=(dp, peer), device_id_type=MESH,
+        )
+
+    def direct(h):
+        return remote(x_out.at[h], near_in.at[h], near_send.at[h], near_recv.at[h], near)
+
+    def via(h):
+        return remote(x_out.at[h], relay_in.at[h], near_send.at[h], relay_recv.at[h], pair)
+
+    def onward(h):
+        return remote(relay_in.at[h], near_in.at[h], relay_send.at[h], near_recv.at[h], far_to)
+
+    def far(h):
+        return remote(p_raw.at[h], far_in.at[h], far_send.at[h], far_recv.at[h], far_to)
+
+    def across(h):
+        return remote(p_sum.at[h], pair_in.at[h], pair_send.at[h], pair_recv.at[h], pair)
+
+    for part in range(parts):
+        for i in (0, 1):
+            load(i, part, q_hbm, landing[i]).wait()
+        widen(part, (xa_in, o1), (xb_in, o2))
+
+    pl.semaphore_wait(
+        barrier, 1 + near_ok.astype(jnp.int32) + far_to_ok.astype(jnp.int32) + far_from_ok.astype(jnp.int32)
+    )
+
+    def x_state(h, _):
+        spot = pl.ds(h, rows, stride=heads)
+        xa = o1[spot, :].astype(jnp.bfloat16)
+        xb = o2[spot, :].astype(jnp.bfloat16)
+        xa_h[h] = xa
+        xb_h[h] = xb
+        x_out[h] = dot(xa * x_rows[...], xb, 0, 0)
+
+        @pl.when(my_turn(h))
+        def _():
+            via(h).start()
+
+        @pl.when(near_ok & jnp.logical_not(my_turn(h)))
+        def _():
+            direct(h).start()
+
+        return 0
+
+    lax.fori_loop(0, heads, x_state, 0)
+
+    p_rows[...] = jnp.where((pos >= p_low) & (pos < p_high), 1.0, 0.0).astype(jnp.bfloat16)
+    in_head, in_tail = pos < head_end, pos >= last_start
+    head_scale = jnp.where(in_head, factor, 0.0).astype(jnp.float32)
+    tail_scale = jnp.where(in_tail, factor, 0.0).astype(jnp.float32)
+    x_scale[...] = jnp.where(odd, tail_scale, head_scale)
+    p_scale[...] = jnp.where(odd, head_scale, tail_scale)
+    col = first + lax.broadcasted_iota(jnp.int32, (1, rows), 1)
+    begin = jnp.zeros((1, rows), jnp.int32)
+    finish = jnp.full((1, rows), big, jnp.int32)
+    for e in ends:
+        begin = jnp.maximum(begin, jnp.where(col >= e, e, zero))
+        finish = jnp.minimum(finish, jnp.where(col < e, e, big))
+    low, high = jnp.where(odd, begin, col), jnp.where(odd, col + 1, finish)
+    row = first + lax.broadcasted_iota(jnp.int32, (rows, rows), 0)
+    mask[...] = jnp.where((row >= low) & (row < high), factor, 0.0).astype(jnp.float32)
+
+    for part in range(parts):
+        for i in (2, 3):
+            load(i, part, q_hbm, landing[i]).wait()
+        widen(part, (pa_in, o3), (pb_in, o4))
+
+    def p_state(h):
+        spot = pl.ds(h, rows, stride=heads)
+        pa = o3[spot, :].astype(jnp.bfloat16)
+        pb = o4[spot, :].astype(jnp.bfloat16)
+        pa_h[h] = pa
+        pb_h[h] = pb
+        p_raw[h] = dot(pa * p_rows[...], pb, 0, 0)
+
+        @pl.when(far_to_ok)
+        def _():
+            far(h).start()
+
+    def relay(h):
+        @pl.when(their_turn(h))
+        def _():
+            remote(x_out.at[h], relay_in.at[h], near_send.at[h], relay_recv.at[h], pair).wait_recv()
+            onward(h).start()
+
+    def inner(h):
+        @pl.when(near_ok)
+        def _():
+            direct(h).wait_recv()
+
+        p_sum[h] = p_raw[h] + jnp.where(p_keep, near_in[h], 0.0)
+        across(h).start()
+
+        @pl.when(far_from_ok)
+        def _():
+            far(h).wait_recv()
+
+        close = (near_in[h] + jnp.where(x_keep, far_in[h], 0.0)).astype(jnp.bfloat16)
+        xa, xb, pa, pb = xa_h[h], xb_h[h], pa_h[h], pb_h[h]
+        m = mask[...]
+        w1 = (m * dot(xa, pa, 1, 1)).astype(jnp.bfloat16)
+        w2 = (m * dot(xb, pb, 1, 1)).astype(jnp.bfloat16)
+        spot = pl.ds(h, rows, stride=heads)
+        scale = x_scale[...]
+        o1[spot, :] = dot(w1, pb, 1, 0) + scale * dot(xa, close, 1, 0)
+        o2[spot, :] = dot(w2, pa, 1, 0) + scale * dot(xb, close, 1, 1)
+        o3[spot, :] = dot(w2, xa, 0, 0)
+        o4[spot, :] = dot(w1, xb, 0, 0)
+
+    def outer(h):
+        across(h).wait_recv()
+        other = pair_in[h].astype(jnp.bfloat16)
+        pa, pb = pa_h[h], pb_h[h]
+        spot = pl.ds(h, rows, stride=heads)
+        scale = p_scale[...]
+        o3[spot, :] = o3[spot, :] + scale * dot(pb, other, 1, 1)
+        o4[spot, :] = o4[spot, :] + scale * dot(pa, other, 1, 0)
+
+    inner_lag, outer_lag = INNER_LAG, OUTER_LAG
+
+    def turn(i, _):
+        @pl.when(i < heads)
+        def _():
+            p_state(i)
+            relay(i)
+
+        @pl.when((i >= inner_lag) & (i < heads + inner_lag))
+        def _():
+            inner(i - inner_lag)
+
+        @pl.when(i >= outer_lag)
+        def _():
+            outer(i - outer_lag)
+
+        return 0
+
+    lax.fori_loop(0, heads + outer_lag, turn, 0)
+
+    def drain(h, _):
+        across(h).wait_send()
+
+        @pl.when(near_ok)
+        def _():
+            direct(h).wait_send()
+
+        @pl.when(far_to_ok)
+        def _():
+            far(h).wait_send()
+
+        @pl.when(their_turn(h))
+        def _():
+            onward(h).wait_send()
+
+        return 0
+
+    lax.fori_loop(0, heads, drain, 0)
+
+
+def settle(i1, i2, i3, i4, att, gq, gk, gv, s1, s2, s3, s4, sem):
+    rows, heads, width = s1.shape
+    parts = sem.shape[1]
+    span = rows // parts
+    step = 16
+    odd = lax.rem(lax.axis_index("seq"), 2) == 1
+    stages = (s1, s2, s3, s4)
+    forward, reverse = (att, gq, gk, gv), (gv, gk, gq, att)
+
+    def put(i, part, dst):
+        cut = pl.ds(part * span, span)
+        return pltpu.make_async_copy(stages[i].at[cut], dst.at[cut], sem.at[i, part])
+
+    for part in range(parts):
+        def narrow(i, _):
+            at = pl.multiple_of(part * span + i * step, step)
+            for src, dst in zip((i1, i2, i3, i4), stages):
+                block = src[pl.ds(at * heads, step * heads), :].reshape(step, heads, width)
+                dst[pl.ds(at, step)] = block.astype(jnp.bfloat16)
+            return 0
+
+        lax.fori_loop(0, span // step, narrow, 0)
+
+        @pl.when(odd)
+        def _():
+            for i in range(4):
+                put(i, part, reverse[i]).start()
+
+        @pl.when(jnp.logical_not(odd))
+        def _():
+            for i in range(4):
+                put(i, part, forward[i]).start()
+
+    for part in range(parts):
+        for i in range(4):
+            put(i, part, att).wait()
+
+
+def local_paired(seq, queries, keys, values, cotangent, doc_lengths):
+    rows, heads, width = queries.shape
+    vmem = pl.BlockSpec(memory_space=pltpu.VMEM)
+    hbm = pl.BlockSpec(memory_space=pltpu.HBM)
+    whole = pltpu.VMEM((rows, heads, width), jnp.bfloat16)
+    by_head = pltpu.VMEM((heads, rows, width), jnp.bfloat16)
+    square = pltpu.VMEM((heads, width, width), jnp.float32)
+    flat = jax.ShapeDtypeStruct((rows * heads, width), jnp.float32)
+    each = pltpu.SemaphoreType.DMA((heads,))
+    held = pl.pallas_call(
+        functools.partial(paired, seq),
+        out_shape=[flat] * 4,
+        in_specs=[hbm] * 5,
+        out_specs=[vmem] * 4,
+        scratch_shapes=[pltpu.SMEM(doc_lengths.shape, jnp.int32)]
+        + [whole] * 4
+        + [by_head] * 4
+        + [pltpu.VMEM((rows, rows), jnp.float32)]
+        + [pltpu.VMEM((rows, width), jnp.bfloat16)] * 2
+        + [pltpu.VMEM((rows, width), jnp.float32)] * 2
+        + [square] * 7
+        + [pltpu.SemaphoreType.DMA, pltpu.SemaphoreType.DMA((4, LOAD_PARTS))]
+        + [each] * 8,
+        compiler_params=pltpu.CompilerParams(
+            collective_id=0, has_side_effects=True, vmem_limit_bytes=40 * 2**20
+        ),
+    )(*(pltpu.with_memory_space_constraint(a, pltpu.HBM) for a in (doc_lengths, queries, keys, values, cotangent)))
+    return pl.pallas_call(
+        settle,
+        out_shape=[jax.ShapeDtypeStruct(queries.shape, jnp.bfloat16)] * 4,
+        in_specs=[vmem] * 4,
+        out_specs=[hbm] * 4,
+        scratch_shapes=[whole] * 4 + [pltpu.SemaphoreType.DMA((4, STORE_PARTS))],
+        compiler_params=pltpu.CompilerParams(vmem_limit_bytes=24 * 2**20),
+    )(*held)
+
+
 def local(seq, queries, keys, values, cotangent, doc_lengths):
     rows, heads, width = queries.shape
     longest = seq * rows // LONGEST_PART
     hops = min(seq - 1, (longest - 1 + rows - 1) // rows)
+    if hops == 2 and seq % 2 == 0:
+        return local_paired(seq, queries, keys, values, cotangent, doc_lengths)
     vmem = pl.BlockSpec(memory_space=pltpu.VMEM)
     flat = pltpu.VMEM((rows * heads, width), jnp.float32)
     by_head = pltpu.VMEM((heads, rows, width), jnp.bfloat16)

time: 57.5 us -> 57.3 us (level)
  the two profiles are of different devices: /device:TPU:12 before, /device:TPU:16 now
where the time goes in v1:
time: 57.3 us; the launch traced here: 57.2 us
  Pallas kernels  56.5 us (99%)
  between operations  0.64 us (1%)
    pallas_call x1, Pallas kernels, local_paired(): pl.pallas_call(functools.partial(paired, seq), out_shape=[flat] * 4, in_s...  54.3 us
    pallas_call x1, Pallas kernels, local_paired(): pl.pallas_call(settle, out_shape=[jax.ShapeDtypeStruct(queries.shape, jnp...  2.26 us

profile of v1, /device:TPU:16, one launch (start us, length us, event | category | flops | bytes accessed | tf_op | source)
XLA Modules:
  0.0 57.2 jit_solution(15487060495328703590)
XLA Ops:
  0.6 54.3 %shard_map.84 = (f32[4096,128]{1,0:T(8,128)S(1)}, f32[4096,128]{1,0:T(8,128)S(1)}, f32[4096,128]{1,0:T(8,128)S(1)}, f32[4096,128]{1,0:T(8,128)S(1)}) custom-call(s32[24]{0:T(128)} %lens_hbm.1, bf16[256,16,128]{2,1,0:T(8,128)(2,1)} %q_hbm.1, bf16[256,16,128]{2,1,0:T(8,128)(2,1)} %k_hbm.1, bf16[256,16,128]{2,1,0:T(8,128)(2,1)} %v_hbm.1, ...), custom_call_target="tpu_custom_call" | custom-call | tf_op jit(solution)/shard_map/pallas_call | solution.py:693
  54.9 2.3 %shard_map.85 = (bf16[256,16,128]{2,1,0:T(8,128)(2,1)}, bf16[256,16,128]{2,1,0:T(8,128)(2,1)}, bf16[256,16,128]{2,1,0:T(8,128)(2,1)}, bf16[256,16,128]{2,1,0:T(8,128)(2,1)}) custom-call(f32[4096,128]{1,0:T(8,128)S(1)} %get-tuple-element.8.i1, f32[4096,128]{1,0:T(8,128)S(1)} %get-tuple-element.9.i2, f32[4096,128]{1,0:T(8,128)S(1)} %get-tuple-element.10.i3, ...), custom_call_target="tpu_custom_call" | custom-call | tf_op jit(solution)/shard_map/pallas_call | solution.py:711

commit v2 on v1

--- a/solution.py
+++ b/solution.py
@@ -367,7 +367,7 @@
     o1, o2, o3, o4,
     lengths, xa_in, xb_in, pa_in, pb_in, xa_h, xb_h, pa_h, pb_h,
     mask, x_rows, p_rows, x_scale, p_scale,
-    x_out, p_raw, p_sum, near_in, far_in, pair_in, relay_in,
+    x_out, p_raw, p_sum, near_in, far_in, pair_in, relay_in, relay_sum,
     len_sem, load_sem, near_send, near_recv, far_send, far_recv,
     pair_send, pair_recv, relay_send, relay_recv,
 ):
@@ -452,6 +452,7 @@
     last_start, last_end = start_of(last), end_of(last)
     x_keep = jnp.where(odd, last_end >= last + rows + 1, head_start <= first - rows)
     p_keep = jnp.where(odd, head_end_prev >= last + 1, tail_start <= first)
+    relay_keep = jnp.where(odd, end_of(first - rows - 1) >= first, start_of(last + rows + 1) <= last + 1)
 
     pos = first + lax.broadcasted_iota(jnp.int32, (rows, width), 0)
     x_low, x_high = jnp.where(odd, tail_start, zero), jnp.where(odd, big, head_end_prev)
@@ -481,6 +482,9 @@
     def their_turn(h):
         return lax.rem(h, levels) < theirs
 
+    def near_turn(h):
+        return lax.rem(h, levels) < jnp.where(odd, level + 1, levels - level)
+
     def remote(src, dst, send, recv, peer):
         return pltpu.make_async_remote_copy(
             src_ref=src, dst_ref=dst, send_sem=send, recv_sem=recv,
@@ -494,7 +498,7 @@
         return remote(x_out.at[h], relay_in.at[h], near_send.at[h], relay_recv.at[h], pair)
 
     def onward(h):
-        return remote(relay_in.at[h], near_in.at[h], relay_send.at[h], near_recv.at[h], far_to)
+        return remote(relay_sum.at[h], near_in.at[h], relay_send.at[h], near_recv.at[h], far_to)
 
     def far(h):
         return remote(p_raw.at[h], far_in.at[h], far_send.at[h], far_recv.at[h], far_to)
@@ -560,7 +564,7 @@
         pb_h[h] = pb
         p_raw[h] = dot(pa * p_rows[...], pb, 0, 0)
 
-        @pl.when(far_to_ok)
+        @pl.when(far_to_ok & jnp.logical_not(their_turn(h)))
         def _():
             far(h).start()
 
@@ -568,6 +572,7 @@
         @pl.when(their_turn(h))
         def _():
             remote(x_out.at[h], relay_in.at[h], near_send.at[h], relay_recv.at[h], pair).wait_recv()
+            relay_sum[h] = relay_in[h] + jnp.where(relay_keep, p_raw[h], 0.0)
             onward(h).start()
 
     def inner(h):
@@ -578,11 +583,11 @@
         p_sum[h] = p_raw[h] + jnp.where(p_keep, near_in[h], 0.0)
         across(h).start()
 
-        @pl.when(far_from_ok)
+        @pl.when(far_from_ok & jnp.logical_not(near_turn(h)))
         def _():
             far(h).wait_recv()
 
-        close = (near_in[h] + jnp.where(x_keep, far_in[h], 0.0)).astype(jnp.bfloat16)
+        close = (near_in[h] + jnp.where(x_keep & jnp.logical_not(near_turn(h)), far_in[h], 0.0)).astype(jnp.bfloat16)
         xa, xb, pa, pb = xa_h[h], xb_h[h], pa_h[h], pb_h[h]
         m = mask[...]
         w1 = (m * dot(xa, pa, 1, 1)).astype(jnp.bfloat16)
@@ -630,7 +635,7 @@
         def _():
             direct(h).wait_send()
 
-        @pl.when(far_to_ok)
+        @pl.when(far_to_ok & jnp.logical_not(their_turn(h)))
         def _():
             far(h).wait_send()
 
@@ -701,7 +706,7 @@
         + [pltpu.VMEM((rows, rows), jnp.float32)]
         + [pltpu.VMEM((rows, width), jnp.bfloat16)] * 2
         + [pltpu.VMEM((rows, width), jnp.float32)] * 2
-        + [square] * 7
+        + [square] * 8
         + [pltpu.SemaphoreType.DMA, pltpu.SemaphoreType.DMA((4, LOAD_PARTS))]
         + [each] * 8,
         compiler_params=pltpu.CompilerParams(

time: 57.3 us -> 52.1 us (0.909)
  the two profiles are of different devices: /device:TPU:16 before, /device:TPU:0 now
where the time goes in v2:
time: 52.1 us; the launch traced here: 52 us
  Pallas kernels  51.4 us (99%)
  between operations  0.64 us (1%)
    pallas_call x1, Pallas kernels, local_paired(): pl.pallas_call(functools.partial(paired, seq), out_shape=[flat] * 4, in_s...  49.1 us
    pallas_call x1, Pallas kernels, local_paired(): pl.pallas_call(settle, out_shape=[jax.ShapeDtypeStruct(queries.shape, jnp...  2.26 us

profile of v2, /device:TPU:0, one launch (start us, length us, event | category | flops | bytes accessed | tf_op | source)
XLA Modules:
  0.0 52.0 jit_solution(16319543394119188595)
XLA Ops:
  0.6 49.1 %shard_map.84 = (f32[4096,128]{1,0:T(8,128)S(1)}, f32[4096,128]{1,0:T(8,128)S(1)}, f32[4096,128]{1,0:T(8,128)S(1)}, f32[4096,128]{1,0:T(8,128)S(1)}) custom-call(s32[24]{0:T(128)} %lens_hbm.1, bf16[256,16,128]{2,1,0:T(8,128)(2,1)} %q_hbm.1, bf16[256,16,128]{2,1,0:T(8,128)(2,1)} %k_hbm.1, bf16[256,16,128]{2,1,0:T(8,128)(2,1)} %v_hbm.1, ...), custom_call_target="tpu_custom_call" | custom-call | tf_op jit(solution)/shard_map/pallas_call | solution.py:698
  49.7 2.3 %shard_map.85 = (bf16[256,16,128]{2,1,0:T(8,128)(2,1)}, bf16[256,16,128]{2,1,0:T(8,128)(2,1)}, bf16[256,16,128]{2,1,0:T(8,128)(2,1)}, bf16[256,16,128]{2,1,0:T(8,128)(2,1)}) custom-call(f32[4096,128]{1,0:T(8,128)S(1)} %get-tuple-element.8.i1, f32[4096,128]{1,0:T(8,128)S(1)} %get-tuple-element.9.i2, f32[4096,128]{1,0:T(8,128)S(1)} %get-tuple-element.10.i3, ...), custom_call_target="tpu_custom_call" | custom-call | tf_op jit(solution)/shard_map/pallas_call | solution.py:716

commit v3 on v2

--- a/solution.py
+++ b/solution.py
@@ -10,8 +10,8 @@
 BLOCK = 256
 LONGEST_PART = 4
 MESH = pl.DeviceIdType.MESH
-INNER_LAG, OUTER_LAG = 3, 5
-LOAD_PARTS, STORE_PARTS = 4, 4
+INNER_LAG, OUTER_LAG = 6, 9
+LOAD_PARTS, STORE_PARTS = 2, 4
 
 
 def dot(a, b, ca, cb):
@@ -368,8 +368,8 @@
     lengths, xa_in, xb_in, pa_in, pb_in, xa_h, xb_h, pa_h, pb_h,
     mask, x_rows, p_rows, x_scale, p_scale,
     x_out, p_raw, p_sum, near_in, far_in, pair_in, relay_in, relay_sum,
-    len_sem, load_sem, near_send, near_recv, far_send, far_recv,
-    pair_send, pair_recv, relay_send, relay_recv,
+    len_sem, load_sem, near_send, far_send, pair_send,
+    near_recv, far_recv, pair_recv, relay_recv,
 ):
     rows, heads, width = xa_in.shape
     factor = (width * BLOCK) ** (-0.5)
@@ -379,6 +379,18 @@
     toward = jnp.where(odd, 1, -1)
     first = me * rows
     last = first + rows - 1
+    near, pair = me + toward, me - toward
+    far_to, far_from = me - 2 * toward, me + 2 * toward
+    near_ok = (near >= 0) & (near < seq)
+    far_to_ok = (far_to >= 0) & (far_to < seq)
+    far_from_ok = (far_from >= 0) & (far_from < seq)
+
+    barrier = pltpu.get_barrier_semaphore()
+    for ok, peer in ((near_ok, near), (pair >= 0, pair), (far_to_ok, far_to), (far_from_ok, far_from)):
+        @pl.when(ok)
+        def _(peer=peer):
+            pl.semaphore_signal(barrier, inc=1, device_id=(dp, peer), device_id_type=MESH)
+
     parts = load_sem.shape[1]
     span = rows // parts
 
@@ -404,26 +416,6 @@
             for part in range(parts):
                 for i in (pair, pair + 1):
                     load(i, part, (k_hbm, v_hbm, q_hbm, c_hbm)[i], landing[i]).start()
-
-    near, pair = me + toward, me - toward
-    far_to, far_from = me - 2 * toward, me + 2 * toward
-    near_ok = (near >= 0) & (near < seq)
-    far_to_ok = (far_to >= 0) & (far_to < seq)
-    far_from_ok = (far_from >= 0) & (far_from < seq)
-
-    barrier = pltpu.get_barrier_semaphore()
-    for ok, peer in ((near_ok, near), (pair >= 0, pair), (far_to_ok, far_to), (far_from_ok, far_from)):
-        @pl.when(ok)
-        def _(peer=peer):
-            pl.semaphore_signal(barrier, inc=1, device_id=(dp, peer), device_id_type=MESH)
-
-    @pl.when(jnp.logical_not(near_ok))
-    def _():
-        near_in[...] = jnp.zeros(near_in.shape, near_in.dtype)
-
-    @pl.when(jnp.logical_not(far_from_ok))
-    def _():
-        far_in[...] = jnp.zeros(far_in.shape, far_in.dtype)
 
     len_load.wait()
     big = jnp.int32(2**30)
@@ -492,19 +484,19 @@
         )
 
     def direct(h):
-        return remote(x_out.at[h], near_in.at[h], near_send.at[h], near_recv.at[h], near)
+        return remote(x_out.at[h], near_in.at[h], near_send, near_recv.at[h], near)
 
     def via(h):
-        return remote(x_out.at[h], relay_in.at[h], near_send.at[h], relay_recv.at[h], pair)
+        return remote(x_out.at[h], relay_in.at[h], near_send, relay_recv.at[h], pair)
 
     def onward(h):
-        return remote(relay_sum.at[h], near_in.at[h], relay_send.at[h], near_recv.at[h], far_to)
+        return remote(relay_sum.at[h], near_in.at[h], far_send, near_recv.at[h], far_to)
 
     def far(h):
-        return remote(p_raw.at[h], far_in.at[h], far_send.at[h], far_recv.at[h], far_to)
+        return remote(p_raw.at[h], far_in.at[h], far_send, far_recv.at[h], far_to)
 
     def across(h):
-        return remote(p_sum.at[h], pair_in.at[h], pair_send.at[h], pair_recv.at[h], pair)
+        return remote(p_sum.at[h], pair_in.at[h], pair_send, pair_recv.at[h], pair)
 
     for part in range(parts):
         for i in (0, 1):
@@ -521,7 +513,10 @@
         xb = o2[spot, :].astype(jnp.bfloat16)
         xa_h[h] = xa
         xb_h[h] = xb
-        x_out[h] = dot(xa * x_rows[...], xb, 0, 0)
+
+        @pl.when(near_ok)
+        def _():
+            x_out[h] = dot(xa * x_rows[...], xb, 0, 0)
 
         @pl.when(my_turn(h))
         def _():
@@ -571,7 +566,7 @@
     def relay(h):
         @pl.when(their_turn(h))
         def _():
-            remote(x_out.at[h], relay_in.at[h], near_send.at[h], relay_recv.at[h], pair).wait_recv()
+            remote(x_out.at[h], relay_in.at[h], near_send, relay_recv.at[h], pair).wait_recv()
             relay_sum[h] = relay_in[h] + jnp.where(relay_keep, p_raw[h], 0.0)
             onward(h).start()
 
@@ -580,14 +575,16 @@
         def _():
             direct(h).wait_recv()
 
-        p_sum[h] = p_raw[h] + jnp.where(p_keep, near_in[h], 0.0)
+        from_near = jnp.where(near_ok, near_in[h], 0.0)
+        p_sum[h] = p_raw[h] + jnp.where(p_keep, from_near, 0.0)
         across(h).start()
 
         @pl.when(far_from_ok & jnp.logical_not(near_turn(h)))
         def _():
             far(h).wait_recv()
 
-        close = (near_in[h] + jnp.where(x_keep & jnp.logical_not(near_turn(h)), far_in[h], 0.0)).astype(jnp.bfloat16)
+        use_far = x_keep & far_from_ok & jnp.logical_not(near_turn(h))
+        close = (from_near + jnp.where(use_far, far_in[h], 0.0)).astype(jnp.bfloat16)
         xa, xb, pa, pb = xa_h[h], xb_h[h], pa_h[h], pb_h[h]
         m = mask[...]
         w1 = (m * dot(xa, pa, 1, 1)).astype(jnp.bfloat16)
@@ -628,24 +625,15 @@
 
     lax.fori_loop(0, heads + outer_lag, turn, 0)
 
-    def drain(h, _):
-        across(h).wait_send()
-
-        @pl.when(near_ok)
-        def _():
-            direct(h).wait_send()
-
-        @pl.when(far_to_ok & jnp.logical_not(their_turn(h)))
-        def _():
-            far(h).wait_send()
-
-        @pl.when(their_turn(h))
-        def _():
-            onward(h).wait_send()
-
-        return 0
-
-    lax.fori_loop(0, heads, drain, 0)
+    remote(p_sum, pair_in, pair_send, pair_recv.at[0], pair).wait_send()
+
+    @pl.when(near_ok)
+    def _():
+        remote(x_out, near_in, near_send, near_recv.at[0], near).wait_send()
+
+    @pl.when(far_to_ok)
+    def _():
+        remote(p_raw, far_in, far_send, far_recv.at[0], far_to).wait_send()
 
 
 def settle(i1, i2, i3, i4, att, gq, gk, gv, s1, s2, s3, s4, sem):
@@ -708,7 +696,8 @@
         + [pltpu.VMEM((rows, width), jnp.float32)] * 2
         + [square] * 8
         + [pltpu.SemaphoreType.DMA, pltpu.SemaphoreType.DMA((4, LOAD_PARTS))]
-        + [each] * 8,
+        + [pltpu.SemaphoreType.DMA] * 3
+        + [each] * 4,
         compiler_params=pltpu.CompilerParams(
             collective_id=0, has_side_effects=True, vmem_limit_bytes=40 * 2**20
         ),

time: 52.1 us -> 49.1 us (0.942)
  Pallas kernels: 51.4 us -> 48.3 us
    pallas_call x1, Pallas kernels: 49.1 us -> 46.1 us  [local_paired(): pl.pallas_call(functools.partial(paired, seq), out_shape=[flat] * 4, in_s...]
where the time goes in v3:
time: 49.1 us; the launch traced here: 49 us
  Pallas kernels  48.3 us (98%)
  between operations  0.64 us (1%)
    pallas_call x1, Pallas kernels, local_paired(): pl.pallas_call(functools.partial(paired, seq), out_shape=[flat] * 4, in_s...  46.1 us
    pallas_call x1, Pallas kernels, local_paired(): pl.pallas_call(settle, out_shape=[jax.ShapeDtypeStruct(queries.shape, jnp...  2.26 us

profile of v3, /device:TPU:0, one launch (start us, length us, event | category | flops | bytes accessed | tf_op | source)
XLA Modules:
  0.0 49.0 jit_solution(6628793317876248450)
XLA Ops:
  0.6 46.1 %shard_map.84 = (f32[4096,128]{1,0:T(8,128)S(1)}, f32[4096,128]{1,0:T(8,128)S(1)}, f32[4096,128]{1,0:T(8,128)S(1)}, f32[4096,128]{1,0:T(8,128)S(1)}) custom-call(s32[24]{0:T(128)} %lens_hbm.1, bf16[256,16,128]{2,1,0:T(8,128)(2,1)} %q_hbm.1, bf16[256,16,128]{2,1,0:T(8,128)(2,1)} %k_hbm.1, bf16[256,16,128]{2,1,0:T(8,128)(2,1)} %v_hbm.1, ...), custom_call_target="tpu_custom_call" | custom-call | tf_op jit(solution)/shard_map/pallas_call | solution.py:686
  46.7 2.3 %shard_map.85 = (bf16[256,16,128]{2,1,0:T(8,128)(2,1)}, bf16[256,16,128]{2,1,0:T(8,128)(2,1)}, bf16[256,16,128]{2,1,0:T(8,128)(2,1)}, bf16[256,16,128]{2,1,0:T(8,128)(2,1)}) custom-call(f32[4096,128]{1,0:T(8,128)S(1)} %get-tuple-element.8.i1, f32[4096,128]{1,0:T(8,128)S(1)} %get-tuple-element.9.i2, f32[4096,128]{1,0:T(8,128)S(1)} %get-tuple-element.10.i3, ...), custom_call_target="tpu_custom_call" | custom-call | tf_op jit(solution)/shard_map/pallas_call | solution.py:705

commit v4 on v3

--- a/solution.py
+++ b/solution.py
@@ -369,7 +369,7 @@
     mask, x_rows, p_rows, x_scale, p_scale,
     x_out, p_raw, p_sum, near_in, far_in, pair_in, relay_in, relay_sum,
     len_sem, load_sem, near_send, far_send, pair_send,
-    near_recv, far_recv, pair_recv, relay_recv,
+    near_recv, side_recv, pair_recv,
 ):
     rows, heads, width = xa_in.shape
     factor = (width * BLOCK) ** (-0.5)
@@ -468,14 +468,19 @@
     mine = jnp.where(odd, levels - 1 - level, level)
     theirs = levels - 1 - mine
 
+    eased = (dp == 0) & even
+
     def my_turn(h):
-        return lax.rem(h, levels) < mine
+        kept = (dp > 0) | even | (level > 0) | (h != heads - 2)
+        return (lax.rem(h, levels) < mine) & kept
 
     def their_turn(h):
-        return lax.rem(h, levels) < theirs
+        kept = jnp.logical_not(eased & (level == 0) & (h == heads - 2))
+        return (lax.rem(h, levels) < theirs) & kept
 
     def near_turn(h):
-        return lax.rem(h, levels) < jnp.where(odd, level + 1, levels - level)
+        kept = jnp.logical_not(eased & (level == 1) & (h == heads - 2))
+        return (lax.rem(h, levels) < jnp.where(odd, level + 1, levels - level)) & kept
 
     def remote(src, dst, send, recv, peer):
         return pltpu.make_async_remote_copy(
@@ -487,13 +492,13 @@
         return remote(x_out.at[h], near_in.at[h], near_send, near_recv.at[h], near)
 
     def via(h):
-        return remote(x_out.at[h], relay_in.at[h], near_send, relay_recv.at[h], pair)
+        return remote(x_out.at[h], relay_in.at[h], near_send, side_recv.at[h], pair)
 
     def onward(h):
         return remote(relay_sum.at[h], near_in.at[h], far_send, near_recv.at[h], far_to)
 
     def far(h):
-        return remote(p_raw.at[h], far_in.at[h], far_send, far_recv.at[h], far_to)
+        return remote(p_raw.at[h], far_in.at[h], far_send, side_recv.at[h], far_to)
 
     def across(h):
         return remote(p_sum.at[h], pair_in.at[h], pair_send, pair_recv.at[h], pair)
@@ -566,7 +571,7 @@
     def relay(h):
         @pl.when(their_turn(h))
         def _():
-            remote(x_out.at[h], relay_in.at[h], near_send, relay_recv.at[h], pair).wait_recv()
+            remote(x_out.at[h], relay_in.at[h], near_send, side_recv.at[h], pair).wait_recv()
             relay_sum[h] = relay_in[h] + jnp.where(relay_keep, p_raw[h], 0.0)
             onward(h).start()
 
@@ -633,7 +638,7 @@
 
     @pl.when(far_to_ok)
     def _():
-        remote(p_raw, far_in, far_send, far_recv.at[0], far_to).wait_send()
+        remote(p_raw, far_in, far_send, side_recv.at[0], far_to).wait_send()
 
 
 def settle(i1, i2, i3, i4, att, gq, gk, gv, s1, s2, s3, s4, sem):
@@ -697,7 +702,7 @@
         + [square] * 8
         + [pltpu.SemaphoreType.DMA, pltpu.SemaphoreType.DMA((4, LOAD_PARTS))]
         + [pltpu.SemaphoreType.DMA] * 3
-        + [each] * 4,
+        + [each] * 3,
         compiler_params=pltpu.CompilerParams(
             collective_id=0, has_side_effects=True, vmem_limit_bytes=40 * 2**20
         ),

time: 49.1 us -> 48.3 us (0.984)
  Pallas kernels: 48.3 us -> 47.5 us
    pallas_call x1, Pallas kernels: 46.1 us -> 45.2 us  [local_paired(): pl.pallas_call(functools.partial(paired, seq), out_shape=[flat] * 4, in_s...]
where the time goes in v4:
time: 48.3 us; the launch traced here: 48.1 us
  Pallas kernels  47.5 us (98%)
  between operations  0.64 us (1%)
    pallas_call x1, Pallas kernels, local_paired(): pl.pallas_call(functools.partial(paired, seq), out_shape=[flat] * 4, in_s...  45.2 us
    pallas_call x1, Pallas kernels, local_paired(): pl.pallas_call(settle, out_shape=[jax.ShapeDtypeStruct(queries.shape, jnp...  2.26 us

profile of v4, /device:TPU:0, one launch (start us, length us, event | category | flops | bytes accessed | tf_op | source)
XLA Modules:
  0.0 48.1 jit_solution(7366876925685356345)
XLA Ops:
  0.6 45.2 %shard_map.84 = (f32[4096,128]{1,0:T(8,128)S(1)}, f32[4096,128]{1,0:T(8,128)S(1)}, f32[4096,128]{1,0:T(8,128)S(1)}, f32[4096,128]{1,0:T(8,128)S(1)}) custom-call(s32[24]{0:T(128)} %lens_hbm.1, bf16[256,16,128]{2,1,0:T(8,128)(2,1)} %q_hbm.1, bf16[256,16,128]{2,1,0:T(8,128)(2,1)} %k_hbm.1, bf16[256,16,128]{2,1,0:T(8,128)(2,1)} %v_hbm.1, ...), custom_call_target="tpu_custom_call" | custom-call | tf_op jit(solution)/shard_map/pallas_call | solution.py:691
  45.9 2.3 %shard_map.85 = (bf16[256,16,128]{2,1,0:T(8,128)(2,1)}, bf16[256,16,128]{2,1,0:T(8,128)(2,1)}, bf16[256,16,128]{2,1,0:T(8,128)(2,1)}, bf16[256,16,128]{2,1,0:T(8,128)(2,1)}) custom-call(f32[4096,128]{1,0:T(8,128)S(1)} %get-tuple-element.8.i1, f32[4096,128]{1,0:T(8,128)S(1)} %get-tuple-element.9.i2, f32[4096,128]{1,0:T(8,128)S(1)} %get-tuple-element.10.i3, ...), custom_call_target="tpu_custom_call" | custom-call | tf_op jit(solution)/shard_map/pallas_call | solution.py:710

commit v5 on v4

--- a/solution.py
+++ b/solution.py
@@ -610,7 +610,7 @@
         o3[spot, :] = o3[spot, :] + scale * dot(pb, other, 1, 1)
         o4[spot, :] = o4[spot, :] + scale * dot(pa, other, 1, 0)
 
-    inner_lag, outer_lag = INNER_LAG, OUTER_LAG
+    inner_lag, outer_lag = INNER_LAG + 2 * lax.rem(dp, 2), OUTER_LAG + 1
 
     def turn(i, _):
         @pl.when(i < heads)

time: 48.3 us -> 48.2 us (level)
  no operation moved by 1% of the time
where the time goes in v5:
time: 48.2 us; the launch traced here: 47.9 us
  Pallas kernels  47.3 us (98%)
  between operations  0.64 us (1%)
    pallas_call x1, Pallas kernels, local_paired(): pl.pallas_call(functools.partial(paired, seq), out_shape=[flat] * 4, in_s...  45 us
    pallas_call x1, Pallas kernels, local_paired(): pl.pallas_call(settle, out_shape=[jax.ShapeDtypeStruct(queries.shape, jnp...  2.26 us

profile of v5, /device:TPU:0, one launch (start us, length us, event | category | flops | bytes accessed | tf_op | source)
XLA Modules:
  0.0 47.9 jit_solution(12648387495115237265)
XLA Ops:
  0.6 45.0 %shard_map.84 = (f32[4096,128]{1,0:T(8,128)S(1)}, f32[4096,128]{1,0:T(8,128)S(1)}, f32[4096,128]{1,0:T(8,128)S(1)}, f32[4096,128]{1,0:T(8,128)S(1)}) custom-call(s32[24]{0:T(128)} %lens_hbm.1, bf16[256,16,128]{2,1,0:T(8,128)(2,1)} %q_hbm.1, bf16[256,16,128]{2,1,0:T(8,128)(2,1)} %k_hbm.1, bf16[256,16,128]{2,1,0:T(8,128)(2,1)} %v_hbm.1, ...), custom_call_target="tpu_custom_call" | custom-call | tf_op jit(solution)/shard_map/pallas_call | solution.py:691
  45.7 2.3 %shard_map.85 = (bf16[256,16,128]{2,1,0:T(8,128)(2,1)}, bf16[256,16,128]{2,1,0:T(8,128)(2,1)}, bf16[256,16,128]{2,1,0:T(8,128)(2,1)}, bf16[256,16,128]{2,1,0:T(8,128)(2,1)}) custom-call(f32[4096,128]{1,0:T(8,128)S(1)} %get-tuple-element.8.i1, f32[4096,128]{1,0:T(8,128)S(1)} %get-tuple-element.9.i2, f32[4096,128]{1,0:T(8,128)S(1)} %get-tuple-element.10.i3, ...), custom_call_target="tpu_custom_call" | custom-call | tf_op jit(solution)/shard_map/pallas_call | solution.py:710
